TPU v7x, 32 devices: a whole 2x2x4 slice. The times are simulated.
32 devices in a mesh: group: 4 (over y, x), shard: 8 (over z, core).
Axes of the slice: x: 2, y: 2, z: 4, core: 2. Of those that a mesh axis runs over, the one named last changes fastest.
Arguments:
- entity: float32 [16384, 400], P(('group', 'shard')), may hold values from -6 to 6
- entity_state: float32 [16384], P(('group', 'shard')), may hold values from 0.1 to 10
- relation: float32 [1345, 400], replicated, may hold values from -6 to 6
- relation_state: float32 [1345], replicated, may hold values from 10 to 1000
- src_send: int32 [32, 8, 128], P(('group', 'shard')), may hold values from 0 to 511
- dst_send: int32 [32, 8, 128], P(('group', 'shard')), may hold values from 0 to 511
- edge_source: int32 [32768], P(('group', 'shard')), may hold values from 0 to 1023
- edge_relation: int32 [32768], P(('group', 'shard')), may hold values from 0 to 1344
- edge_target: int32 [32768], P(('group', 'shard')), may hold values from 0 to 1023
- neg_slots: int32 [64, 1000], P(('group', 'shard')), may hold values from 0 to 1023
- edge_count: int32 [32], P(('group', 'shard')), may hold values from 1 to 1024, 10922 in all
Outputs:
- entity_new: float32 [16384, 400], P(('group', 'shard'))
- relation_new: float32 [1345, 400], replicated
- edge_loss: float32 [32768], P(('group', 'shard'))
Inputs may be any that keep to these rules, and one draw needn't show every extreme that they name: The live edges of a device are its first edge_count slots; some device has all 1024 live.
All inputs are finite; a program needn't handle non-finite values.
Results may differ from a plain program's by a relative error of at most 0.0003.
Values sent between devices are 32-bit elements; how exact they have to be, the bound alone decides.
No kernel may reach another device: no remote copies, remote signals or barrier semaphores. Data moves between devices by JAX's collectives and lax.ppermute only.
A program may use at most 128 MiB of HBM per device.

v0:
```python
import jax
import jax.numpy as jnp
from jax import lax
from jax.sharding import PartitionSpec as P

SPAN = 512


learn_rate = 0.5


def passed_along(value, axis, by):
    count = lax.axis_size(axis)
    return lax.ppermute(value, axis, [(i, (i + by) % count) for i in range(count)])


def complex_product(multiplier, multiplicand):
    half_width = multiplier.shape[1] // 2
    first_real, first_imag = (multiplier[:, :half_width], multiplier[:, half_width:])
    second_real, second_imag = (multiplicand[:, :half_width], multiplicand[:, half_width:])
    return jnp.concatenate(
        [
            first_real * second_real - first_imag * second_imag,
            first_real * second_imag + first_imag * second_real,
        ],
        axis=1,
    )


def conj_product(multiplier, multiplicand):
    half_width = multiplier.shape[1] // 2
    first_real, first_imag = (multiplier[:, :half_width], multiplier[:, half_width:])
    second_real, second_imag = (multiplicand[:, :half_width], multiplicand[:, half_width:])
    return jnp.concatenate(
        [
            first_real * second_real + first_imag * second_imag,
            first_imag * second_real - first_real * second_imag,
        ],
        axis=1,
    )


def span_terms(queries, tail_rows, negatives, live_mask):
    pos_score = jnp.sum(queries * tail_rows, axis=1)
    neg_score = jnp.dot(queries, negatives.T, precision=lax.Precision.HIGHEST)
    score_peak = jnp.maximum(pos_score, jnp.max(neg_score, axis=1))
    exp_total = jnp.exp(pos_score - score_peak) + jnp.sum(
        jnp.exp(neg_score - score_peak[:, None]), axis=1
    )
    log_total = score_peak + jnp.log(exp_total)
    edge_loss = (log_total - pos_score) * live_mask
    pos_grad = (jnp.exp(pos_score - log_total) - 1.0) * live_mask
    neg_grad = jnp.exp(neg_score - log_total[:, None]) * live_mask[:, None]
    neg_query = jnp.dot(neg_grad, negatives, precision=lax.Precision.HIGHEST)
    negative_grad = lax.dot_general(
        neg_grad, queries, (((0,), (0,)), ((), ())), precision=lax.Precision.HIGHEST
    )
    return (edge_loss, pos_grad, neg_query, negative_grad)


def adagrad(params, accumulator, gradient):
    new_state = accumulator + jnp.mean(gradient * gradient, axis=1)
    return params - learn_rate * gradient / jnp.sqrt(new_state)[:, None]


def on_device(
    entity,
    entity_state,
    relation,
    relation_state,
    src_send,
    dst_send,
    edge_source,
    edge_relation,
    edge_target,
    neg_slots,
    edge_count,
):
    feature_count = entity.shape[1]
    peer_count, block_size = (src_send.shape[1], src_send.shape[2])
    table_rows = peer_count * block_size
    edge_rows = edge_source.shape[0]
    spans = edge_rows // SPAN
    sent_source = lax.all_to_all(
        entity[src_send[0]], "shard", split_axis=0, concat_axis=0, tiled=True
    )
    source_table = sent_source.reshape(table_rows, feature_count)
    shifted = passed_along(entity[dst_send[0]], "group", -1)
    target_blocks = lax.all_to_all(shifted, "shard", split_axis=0, concat_axis=0, tiled=True)
    target_table = target_blocks.reshape(table_rows, feature_count)
    live_count = edge_count[0]
    live_mask = (jnp.arange(edge_rows, dtype=jnp.int32) < live_count).astype(jnp.float32)
    head_rows = source_table[edge_source]
    tail_rows = target_table[edge_target]
    rel_rows = relation[edge_relation]
    queries = complex_product(head_rows, rel_rows)

    def span_turn(position, carried):
        loss_all, pos_all, query_all, target_grad = carried
        first_row = position * SPAN
        slots = neg_slots[position]
        edge_loss, pos_grad, neg_query, negative_grad = span_terms(
            lax.dynamic_slice_in_dim(queries, first_row, SPAN),
            lax.dynamic_slice_in_dim(tail_rows, first_row, SPAN),
            target_table[slots],
            lax.dynamic_slice_in_dim(live_mask, first_row, SPAN),
        )
        loss_all = lax.dynamic_update_slice_in_dim(loss_all, edge_loss, first_row, 0)
        pos_all = lax.dynamic_update_slice_in_dim(pos_all, pos_grad, first_row, 0)
        query_all = lax.dynamic_update_slice_in_dim(query_all, neg_query, first_row, 0)
        target_grad = target_grad.at[slots].add(negative_grad)
        return (loss_all, pos_all, query_all, target_grad)

    initial = (
        jnp.zeros((edge_rows,), jnp.float32),
        jnp.zeros((edge_rows,), jnp.float32),
        jnp.zeros((edge_rows, feature_count), jnp.float32),
        jnp.zeros((table_rows, feature_count), jnp.float32),
    )
    edge_loss, pos_grad, neg_query, target_grad = lax.fori_loop(0, spans, span_turn, initial)
    query_grad = pos_grad[:, None] * tail_rows + neg_query
    target_grad = target_grad.at[edge_target].add(pos_grad[:, None] * queries)
    source_grad = (
        jnp.zeros((table_rows, feature_count), jnp.float32)
        .at[edge_source]
        .add(conj_product(query_grad, rel_rows))
    )
    relation_part = (
        jnp.zeros(relation.shape, jnp.float32)
        .at[edge_relation]
        .add(conj_product(query_grad, head_rows))
    )
    relation_total = lax.psum(relation_part, ("group", "shard"))
    returned_source = lax.all_to_all(
        source_grad.reshape(peer_count, block_size, feature_count),
        "shard",
        split_axis=0,
        concat_axis=0,
        tiled=True,
    )
    entity_grad = (
        jnp.zeros(entity.shape, jnp.float32)
        .at[src_send[0].reshape(-1)]
        .add(returned_source.reshape(-1, feature_count))
    )
    target_blocks_grad = target_grad.reshape(peer_count, block_size, feature_count)
    returned_blocks = lax.all_to_all(
        target_blocks_grad, "shard", split_axis=0, concat_axis=0, tiled=True
    )
    home_blocks = passed_along(returned_blocks, "group", 1)
    entity_grad = entity_grad.at[dst_send[0].reshape(-1)].add(
        home_blocks.reshape(-1, feature_count)
    )
    return (
        adagrad(entity, entity_state, entity_grad),
        adagrad(relation, relation_state, relation_total),
        edge_loss,
    )


def solution(mesh):
    return jax.shard_map(
        on_device,
        mesh=mesh,
        in_specs=(
            P(("group", "shard"), None),
            P(("group", "shard")),
            P(),
            P(),
            P(("group", "shard"), None, None),
            P(("group", "shard"), None, None),
            P(("group", "shard")),
            P(("group", "shard")),
            P(("group", "shard")),
            P(("group", "shard"), None),
            P(("group", "shard")),
        ),
        out_specs=(P(("group", "shard"), None), P(), P(("group", "shard"))),
        check_vma=False,
    )
```

profile of v0, /device:TPU:0, one launch (start us, length us, event | category | flops | bytes accessed | tf_op | source)
XLA Modules:
  0.0 453.1 jit_solution(17644259954135910867)
XLA Ops:
  9.4 3.5 gather_fusion.1
  12.9 1.7 copy.47
  14.6 6.5 %all-to-all-start = ((f32[8,128,400]{1,2,0:T(8,128)}), f32[8,128,400]{1,2,0:T(8,128)}, u32[]{:S(2)}, u32[]{:S(2)}) async-start(f32[8,128,400]{1,2,0:T(8,128)} %copy.47), calls=%async_computation | async-start | bytes 3276800 | tf_op jit(solution)/shard_map/all_to_all | solution.py:84
  21.1 3.5 gather_fusion.4
  24.6 1.8 copy.51
  26.4 2.4 collective-permute-start
  28.8 36.1 %collective-permute-done = f32[8,128,400]{1,2,0:T(8,128)} collective-permute-done((f32[8,128,400]{1,2,0:T(8,128)}, f32[8,128,400]{1,2,0:T(8,128)}, u32[]{:S(2)}, u32[]{:S(2)}) %collective-permute-start) | collective-permute-done | bytes 1638432 | tf_op jit(solution)/shard_map/ppermute | solution.py:14
  64.9 4.7 %all-to-all-start.1 = ((f32[8,128,400]{1,2,0:T(8,128)}), f32[8,128,400]{1,2,0:T(8,128)}, u32[]{:S(2)}, u32[]{:S(2)}) async-start(f32[8,128,400]{1,2,0:T(8,128)} %collective-permute-done), calls=%async_computation.1 | async-start | bytes 3276800 | tf_op jit(solution)/shard_map/all_to_all | solution.py:89
  69.6 2.5 copy.49
  72.9 4.9 %gather_fusion.3 = f32[1024,400]{1,0:T(8,128)} fusion(f32[1345,400]{1,0:T(8,128)S(1)} %copy.49, s32[1024]{0:T(1024)S(1)} %get-tuple-element.335), kind=kCustom, calls=%fused_computation.3 | custom fusion | bytes 3280896 | tf_op jit(solution)/shard_map/gather | solution.py:95
  77.8 1.8 copy.48
  79.6 4.9 %gather_fusion.2 = f32[1024,400]{1,0:T(8,128)} fusion(f32[1024,400]{1,0:T(8,128)S(1)} %bitcast.42, s32[1024]{0:T(1024)S(1)} %get-tuple-element.338), kind=kCustom, calls=%fused_computation.2 | custom fusion | bytes 3280896 | tf_op jit(solution)/shard_map/gather | solution.py:93
  84.6 3.1 multiply_subtract_fusion.2
  88.7 1.8 pad_maximum_fusion
  90.5 18.4 %all-to-all-done.1 = f32[8,128,400]{1,2,0:T(8,128)} async-done(((f32[8,128,400]{1,2,0:T(8,128)}), f32[8,128,400]{1,2,0:T(8,128)}, u32[]{:S(2)}, u32[]{:S(2)}) %all-to-all-start.1) | async-done | bytes 1638432 | tf_op jit(solution)/shard_map/all_to_all | solution.py:89
  108.9 1.8 copy.52
  110.8 4.9 %gather_fusion.5 = f32[1024,400]{1,0:T(8,128)} fusion(f32[1024,400]{1,0:T(8,128)S(1)} %bitcast.39, s32[1024]{0:T(1024)S(1)} %get-tuple-element.337), kind=kCustom, calls=%fused_computation.5 | custom fusion | bytes 3280896 | tf_op jit(solution)/shard_map/gather | solution.py:94
  118.7 68.5 %while.21 = (s32[]{:T(128)}, f32[1024]{0:T(1024)S(1)}, f32[1024]{0:T(1024)S(1)}, f32[1024,400]{0,1:T(8,128)}, f32[1024,400]{1,0:T(8,128)}, /*index=5*/f32[1024,4...) while((s32[]{:T(128)}, f32[1024]{0:T(1024)S(1)}, ...), condition=%wide.region_5.0_spmd, body=%wide.region_0.0_spmd.sunk | while | flops 7377200640 | bytes 52573032 | solution.py:120
  120.6 4.9 %gather_fusion = f32[1000,400]{1,0:T(8,128)} fusion(f32[1024,400]{1,0:T(8,128)S(1)} %get-tuple-element.447, s32[1024]{0:T(1024)S(1)} %pad_clamp_fusion.2), kind=kCustom, calls=%fused_computation.clone.1 | custom fusion | bytes 3204000 | tf_op jit(solution)/shard_map/while/body/eval_jaxpr/gather | solution.py:105
  125.5 5.4 %fusion.44 = (f32[512]{0:T(512)S(1)}, f32[512,1000]{0,1:T(8,128)S(1)}) fusion(f32[1000,400]{1,0:T(8,128)} %gather_fusion, f32[1024,400]{1,0:T(8,128)} %get-tuple-element.444, s32[]{:T(128)S(6)} %select_n.125), kind=kOutput, calls=%fused_computation.77.clone.1 | convolution fusion | flops 2458111488 | bytes 5146628 | tf_op jit(solution)/shard_map/while/body/eval_jaxpr/dot_general | solution.py:45
  132.5 4.2 fusion.45
  138.0 4.9 %fusion.46 = f32[1000,400]{1,0:T(8,128)} fusion(f32[512,1000]{0,1:T(8,128)S(1)} %get-tuple-element.407, f32[512]{0:T(512)S(1)} %get-tuple-element.408, f32[512]{0:T(512)S(1)} %get-tuple-element.409, f32[1024,400]{1,0:T(8,128)S(1)} %copy-done.5, s32[]{:T(128)S(6)} %select_n.125), kind=kOutput, calls=%fused_computation.14.clone.1 | convolution fusion | flops 2458624000 | bytes 4700676 | tf_op jit(solution)/shard_map/while/body/eval_jaxpr/dot_general | solution.py:55
  142.8 10.1 %scatter_fusion = f32[1024,400]{1,0:T(8,128)} fusion(f32[1024,400]{1,0:T(8,128)} %get-tuple-element.429, s32[1000]{0:T(1024)S(1)} %bitcast.49, f32[1000,400]{1,0:T(8,128)} %fusion.46), kind=kCustom, calls=%fused_computation.6.clone.1 | custom fusion | flops 400000 | bytes 4804000 | tf_op jit(solution)/shard_map/while/body/eval_jaxpr/scatter-add | solution.py:111
  154.7 4.9 %gather_fusion = f32[1000,400]{1,0:T(8,128)} fusion(f32[1024,400]{1,0:T(8,128)S(1)} %get-tuple-element.447, s32[1024]{0:T(1024)S(1)} %pad_clamp_fusion.2), kind=kCustom, calls=%fused_computation.clone.1 | custom fusion | bytes 3204000 | tf_op jit(solution)/shard_map/while/body/eval_jaxpr/gather | solution.py:105
  159.6 5.4 %fusion.44 = (f32[512]{0:T(512)S(1)}, f32[512,1000]{0,1:T(8,128)S(1)}) fusion(f32[1000,400]{1,0:T(8,128)} %gather_fusion, f32[1024,400]{1,0:T(8,128)} %get-tuple-element.444, s32[]{:T(128)S(6)} %select_n.125), kind=kOutput, calls=%fused_computation.77.clone.1 | convolution fusion | flops 2458111488 | bytes 5146628 | tf_op jit(solution)/shard_map/while/body/eval_jaxpr/dot_general | solution.py:45
  166.6 4.2 fusion.45
  172.1 4.9 %fusion.46 = f32[1000,400]{1,0:T(8,128)} fusion(f32[512,1000]{0,1:T(8,128)S(1)} %get-tuple-element.407, f32[512]{0:T(512)S(1)} %get-tuple-element.408, f32[512]{0:T(512)S(1)} %get-tuple-element.409, f32[1024,400]{1,0:T(8,128)S(1)} %copy-done.5, s32[]{:T(128)S(6)} %select_n.125), kind=kOutput, calls=%fused_computation.14.clone.1 | convolution fusion | flops 2458624000 | bytes 4700676 | tf_op jit(solution)/shard_map/while/body/eval_jaxpr/dot_general | solution.py:55
  176.9 10.1 %scatter_fusion = f32[1024,400]{1,0:T(8,128)} fusion(f32[1024,400]{1,0:T(8,128)} %get-tuple-element.429, s32[1000]{0:T(1024)S(1)} %bitcast.49, f32[1000,400]{1,0:T(8,128)} %fusion.46), kind=kCustom, calls=%fused_computation.6.clone.1 | custom fusion | flops 400000 | bytes 4804000 | tf_op jit(solution)/shard_map/while/body/eval_jaxpr/scatter-add | solution.py:111
  187.3 10.6 %scatter_custom_fusion.3 = f32[1024,400]{1,0:T(8,128)} fusion(f32[1024,400]{1,0:T(8,128)} %get-tuple-element.250, s32[1024]{0:T(1024)S(1)} %get-tuple-element.336, f32[1024]{0:T(1024)S(1)} %get-tuple-element.248, f32[1024,200]{1,0:T(8,128)} %copy-done.9, f32[1024,200]{1,0:T(8,128)S(1)} %get-tuple-element.330), kind=kCustom, calls=%fused_computation.43 | custom fusion | flops 1228800 | bytes 3739648 | tf_op jit(solution)/shard_map/scatter-add | solution.py:122
  197.8 2.8 copy.59
  200.6 4.3 all-to-all-start.3
  205.0 3.0 copy.54
  207.9 2.0 multiply_add_fusion
  210.8 2.5 multiply_add_fusion.1
  213.3 8.1 %scatter_custom_fusion.1 = f32[1024,400]{1,0:T(8,128)S(1)} fusion(s32[1024]{0:T(1024)S(1)} %get-tuple-element.339, f32[1024,200]{1,0:T(8,128)S(1)} %get-tuple-element.332, f32[]{:T(128)} %constant.108, f32[1024,200]{1,0:T(8,128)} %get-tuple-element.333, f32[]{:T(128)} %constant.97.clone.1), kind=kCustom, calls=%fused_computation.35 | custom fusion | flops 819200 | bytes 3506184 | tf_op jit(solution)/shard_map/scatter-add | solution.py:126
  221.4 1.7 copy.55
  223.2 21.0 %all-to-all-done.3 = f32[8,128,400]{1,2,0:T(8,128)} async-done(((f32[8,128,400]{1,2,0:T(8,128)}), f32[8,128,400]{1,2,0:T(8,128)}, u32[]{:S(2)}, u32[]{:S(2)}) %all-to-all-start.3) | async-done | bytes 1638432 | tf_op jit(solution)/shard_map/all_to_all | solution.py:147
  244.2 4.3 all-to-all-start.2
  248.6 9.0 %scatter_custom_fusion.5 = f32[1345,400]{1,0:T(8,128)} fusion(s32[1024]{0:T(1024)S(1)} %get-tuple-element.334, f32[1024,200]{1,0:T(8,128)S(1)} %copy-done.13, f32[]{:T(128)} %constant.108, f32[1024,200]{1,0:T(8,128)S(1)} %copy-done.12, f32[]{:T(128)} %constant.97.clone.1), kind=kCustom, calls=%fused_computation.39 | custom fusion | flops 819200 | bytes 4249160 | tf_op jit(solution)/shard_map/scatter-add | solution.py:131
  257.6 2.4 collective-permute-start.1
  260.1 155.7 %all-reduce.2.cloned.1.call-done = f32[1345,400]{1,0:T(8,128)} async-done(((f32[1345,400]{1,0:T(8,128)}), f32[1345,400]{1,0:T(8,128)}) %all-reduce.2.cloned.1.call-update) | async-done | bytes 2152016 | tf_op jit(solution)/shard_map/psum | solution.py:133
  415.8 2.1 multiply_reduce_fusion.1
  417.9 3.8 divide_subtract_fusion
  421.6 3.3 copy.65
  424.9 1.8 copy.67
  426.7 6.8 %scatter_custom_fusion.2 = f32[512,400]{1,0:T(8,128)S(1)} fusion(s32[1024]{0:T(1024)S(1)} %bitcast.53, f32[1024,400]{1,0:T(8,128)S(1)} %bitcast.47, f32[]{:T(128)} %constant.97.clone.1), kind=kCustom, calls=%fused_computation.57 | custom fusion | flops 409600 | bytes 819204 | tf_op jit(solution)/shard_map/scatter-add | solution.py:144
  433.6 2.8 copy.70
  436.4 7.8 %scatter_fusion.1 = f32[512,400]{1,0:T(8,128)S(1)} fusion(f32[512,400]{1,0:T(8,128)S(1)} %scatter_custom_fusion.2, s32[1024]{0:T(1024)S(1)} %bitcast.50, f32[1024,400]{1,0:T(8,128)} %bitcast.43), kind=kCustom, calls=%fused_computation.10 | custom fusion | flops 409600 | bytes 4919296 | tf_op jit(solution)/shard_map/scatter-add | solution.py:151
  (91 shorter events, 18.0 us)
Async XLA Ops:
  8.6 12.5 %copy-start = (f32[512,400]{1,0:T(8,128)}, f32[512,400]{1,0:T(8,128)S(1)}, u32[]{:S(2)}) copy-start(f32[512,400]{1,0:T(8,128)S(1)} %copy.62) | copy-start | bytes 2457604
  14.6 6.5 %copy-start.16 = (s32[1,8,128]{2,1,0:T(8,128)S(1)}, s32[1,8,128]{2,1,0:T(8,128)}, u32[]{:S(2)}) copy-start(s32[1,8,128]{2,1,0:T(8,128)} %param.18) | copy-start | bytes 12292
  14.6 50.3 %all-to-all-start = ((f32[8,128,400]{1,2,0:T(8,128)}), f32[8,128,400]{1,2,0:T(8,128)}, u32[]{:S(2)}, u32[]{:S(2)}) async-start(f32[8,128,400]{1,2,0:T(8,128)} %copy.47), calls=%async_computation | async-start | bytes 3276800 | tf_op jit(solution)/shard_map/all_to_all | solution.py:84
  26.4 38.5 %collective-permute-start = (f32[8,128,400]{1,2,0:T(8,128)}, f32[8,128,400]{1,2,0:T(8,128)}, u32[]{:S(2)}, u32[]{:S(2)}) collective-permute-start(f32[8,128,400]{1,2,0:T(8,128)} %copy.51), channel_id=1, source_target_pairs={{0,24},{8,0},{16,8},{24,16},{1,25},{9,1},{17,9},{25,17},{2,26},{10... | collective-permute-start | bytes 4915208 | tf_op jit(solution)/shard_map/ppermute | solution.py:14
  64.9 44.0 %all-to-all-start.1 = ((f32[8,128,400]{1,2,0:T(8,128)}), f32[8,128,400]{1,2,0:T(8,128)}, u32[]{:S(2)}, u32[]{:S(2)}) async-start(f32[8,128,400]{1,2,0:T(8,128)} %collective-permute-done), calls=%async_computation.1 | async-start | bytes 3276800 | tf_op jit(solution)/shard_map/all_to_all | solution.py:89
  69.6 3.2 copy-start.18
  72.1 5.6 %copy-start.3 = (f32[1345,400]{1,0:T(8,128)}, f32[1345,400]{1,0:T(8,128)S(1)}, u32[]{:S(2)}) copy-start(f32[1345,400]{1,0:T(8,128)S(1)} %copy.49) | copy-start | bytes 6456004
  72.8 4.9 %copy-start.19 = (s32[1024]{0:T(1024)S(1)}, s32[1024]{0:T(1024)}, u32[]{:S(2)}) copy-start(s32[1024]{0:T(1024)} %param.19) | copy-start | bytes 12292
  72.8 4.9 %copy-start.20 = (s32[1024]{0:T(1024)S(1)}, s32[1024]{0:T(1024)}, u32[]{:S(2)}) copy-start(s32[1024]{0:T(1024)} %param.21) | copy-start | bytes 12292
  87.7 1.0 copy-start.9
  115.6 3.1 copy-start.14
  125.5 6.1 %copy-start.10 = (f32[1024,400]{0,1:T(8,128)S(1)}, f32[1024,400]{0,1:T(8,128)}, u32[]{:S(2)}) copy-start(f32[1024,400]{0,1:T(8,128)} %get-tuple-element.428) | copy-start | bytes 4915204 | tf_op jit(solution)/shard_map/while
  130.9 1.6 copy-start.2
  132.5 5.5 %copy-start.5 = (f32[1024,400]{1,0:T(8,128)S(1)}, f32[1024,400]{1,0:T(8,128)}, u32[]{:S(2)}) copy-start(f32[1024,400]{1,0:T(8,128)} %get-tuple-element.444) | copy-start | bytes 4915204 | tf_op jit(solution)/shard_map/while
  136.7 1.3 copy-start.11
  159.6 6.1 %copy-start.10 = (f32[1024,400]{0,1:T(8,128)S(1)}, f32[1024,400]{0,1:T(8,128)}, u32[]{:S(2)}) copy-start(f32[1024,400]{0,1:T(8,128)} %get-tuple-element.428) | copy-start | bytes 4915204 | tf_op jit(solution)/shard_map/while
  165.0 1.6 copy-start.2
  166.6 5.5 %copy-start.5 = (f32[1024,400]{1,0:T(8,128)S(1)}, f32[1024,400]{1,0:T(8,128)}, u32[]{:S(2)}) copy-start(f32[1024,400]{1,0:T(8,128)} %get-tuple-element.444) | copy-start | bytes 4915204 | tf_op jit(solution)/shard_map/while
  170.8 1.3 copy-start.11
  187.2 10.6 %copy-start.21 = (f32[1024]{0:T(1024)}, f32[1024]{0:T(1024)S(1)}, u32[]{:S(2)}) copy-start(f32[1024]{0:T(1024)S(1)} %get-tuple-element.300) | copy-start | bytes 12292
  200.6 43.5 %all-to-all-start.3 = ((f32[8,128,400]{1,2,0:T(8,128)}), f32[8,128,400]{1,2,0:T(8,128)}, u32[]{:S(2)}, u32[]{:S(2)}) async-start(f32[8,128,400]{1,2,0:T(8,128)} %copy.59), calls=%async_computation.3 | async-start | bytes 3276800 | tf_op jit(solution)/shard_map/all_to_all | solution.py:147
  205.0 3.0 copy-start.6
  207.9 2.2 copy-start.7
  207.9 2.9 copy-start.8
  223.2 25.3 %copy-start.12 = (f32[1024,200]{1,0:T(8,128)S(1)}, f32[1024,200]{1,0:T(8,128)}, u32[]{:S(2)}) copy-start(f32[1024,200]{1,0:T(8,128)} %get-tuple-element.326) | copy-start | bytes 2457604
  223.2 25.3 %copy-start.13 = (f32[1024,200]{1,0:T(8,128)S(1)}, f32[1024,200]{1,0:T(8,128)}, u32[]{:S(2)}) copy-start(f32[1024,200]{1,0:T(8,128)} %get-tuple-element.327) | copy-start | bytes 2457604
  244.2 180.7 %all-to-all-start.2 = ((f32[8,128,400]{1,2,0:T(8,128)}), f32[8,128,400]{1,2,0:T(8,128)}, u32[]{:S(2)}, u32[]{:S(2)}) async-start(f32[8,128,400]{1,2,0:T(8,128)} %copy.55), calls=%async_computation.2 | async-start | bytes 3276800 | tf_op jit(solution)/shard_map/all_to_all | solution.py:134
  248.5 167.3 %all-reduce.2.cloned.1.call-start = ((), (), s32[]{:S(2)}) async-start(), calls=%async_computation.4 | async-start | bytes 5537792 | tf_op jit(solution)/shard_map/psum | solution.py:133
  257.6 2.5 copy-start.15
  257.6 160.3 %copy-start.17 = (f32[1345]{0:T(1024)S(1)}, f32[1345]{0:T(1024)}, u32[]{:S(2)}) copy-start(f32[1345]{0:T(1024)} %param.16) | copy-start | bytes 16144
  257.6 160.3 %copy-start.4 = (f32[1345,400]{1,0:T(8,128)S(1)}, f32[1345,400]{1,0:T(8,128)}, u32[]{:S(2)}) copy-start(f32[1345,400]{1,0:T(8,128)} %copy-done.3) | copy-start | bytes 6456004
  257.6 176.0 %collective-permute-start.1 = (f32[8,128,400]{1,2,0:T(8,128)}, f32[8,128,400]{1,2,0:T(8,128)}, u32[]{:S(2)}, u32[]{:S(2)}) collective-permute-start(f32[8,128,400]{1,2,0:T(8,128)} %all-to-all-done.3), channel_id=1, source_target_pairs={{0,8},{8,16},{16,24},{24,0},{1,9},{9,17},{17,25},{25,1},{2,10},{10... | collective-permute-start | bytes 4915208 | tf_op jit(solution)/shard_map/ppermute | solution.py:14
  436.4 7.9 %copy-start.22 = (f32[512]{0:T(512)S(1)}, f32[512]{0:T(512)}, u32[]{:S(2)}) copy-start(f32[512]{0:T(512)} %param.14) | copy-start | bytes 6148
  436.4 7.9 %copy-start.1 = (f32[512,400]{1,0:T(8,128)S(1)}, f32[512,400]{1,0:T(8,128)}, u32[]{:S(2)}) copy-start(f32[512,400]{1,0:T(8,128)} %copy-done) | copy-start | bytes 2457604
Sparse Core Ops, SparseCore 0:
  257.7 157.9 all-reduce.1
where the time goes:
time: 458 us; the launch traced here: 453 us
  waiting for transfers between devices  231 us (50%)
  other arithmetic  83.7 us (18%)
  local copies, waits for them, and re-layouts  68.6 us (15%)
  matrix products  29 us (6%)
  starting transfers between devices  24.7 us (5%)
  between operations  15.5 us (3%)
    psum x1, waiting for transfers between devices, on_device(): relation_total = lax.psum(relation_part, ('group', 'shard'))  156 us
    ppermute x2, waiting for transfers between devices, passed_along(): lax.ppermute(value, axis, [(i, (i + by) % count) for i in range(count)])  36.1 us
    all_to_all x1, waiting for transfers between devices, on_device(): lax.all_to_all(target_blocks_grad, 'shard', split_axis=0, concat_axis=0,...  21 us
    scatter-add x2, other arithmetic, span_turn(): target_grad = target_grad.at[slots].add(negative_grad)  20.2 us
    all_to_all x1, waiting for transfers between devices, on_device(): lax.all_to_all(shifted, 'shard', split_axis=0, concat_axis=0, tiled=True)  18.4 us
    dot_general x2, matrix products, span_terms(): neg_score = jnp.dot(queries, negatives.T, precision=lax.Precision.HIGHEST)  10.9 us
    scatter-add x1, other arithmetic, on_device(): target_grad = target_grad.at[edge_target].add(pos_grad[:, None] * queries)  10.6 us
    unnamed x42, local copies, waits for them, and re-layouts  10.4 us
  transfers between devices with their start and end apart: 7, of which 4 were waited for; matrix products, arithmetic and copies ran while one was open for 15% of the time, Pallas kernels for 0%

commit v1 on v0

v1 whole, which is shorter than its diff:
```python
import functools

import jax
import jax.numpy as jnp
from jax import lax
from jax.experimental import pallas as pl
from jax.experimental.pallas import tpu as pltpu
from jax.sharding import PartitionSpec as P

SPAN = 512
LANES = 128
CHUNK = 256

learn_rate = 0.5

F32, BF16, I32 = jnp.float32, jnp.bfloat16, jnp.int32
WHOLE = pl.BlockSpec(memory_space=pltpu.VMEM)
VMEM_LIMIT = 60 << 20


def params():
    return pltpu.CompilerParams(vmem_limit_bytes=VMEM_LIMIT, dimension_semantics=("arbitrary",))


def cost(flops, moved):
    return pl.CostEstimate(flops=flops, bytes_accessed=moved, transcendentals=0)


def split2(x):
    hi = x.astype(BF16)
    return hi, (x - hi.astype(F32)).astype(BF16)


def split3(x):
    hi = x.astype(BF16)
    rest = x - hi.astype(F32)
    mid = rest.astype(BF16)
    return hi, mid, (rest - mid.astype(F32)).astype(BF16)


def dot(a, b):
    return jnp.dot(a, b, preferred_element_type=F32)


def dot_nt(a, b):
    return lax.dot_general(a, b, (((1,), (1,)), ((), ())), preferred_element_type=F32)


def one_hot(mask):
    return jnp.where(mask, 1.0, 0.0).astype(BF16)


def rows_hot(length, slots):
    return one_hot(lax.broadcasted_iota(I32, (length, slots.shape[1]), 0) == slots)


def columns_hot(slots, length):
    return one_hot(lax.broadcasted_iota(I32, (slots.shape[0], length), 1) == slots)


def complex_product(a, b):
    half = a.shape[0] // 2
    ar, ai, br, bi = a[:half], a[half:], b[:half], b[half:]
    return jnp.concatenate([ar * br - ai * bi, ar * bi + ai * br], axis=0)


def conj_product(a, b):
    half = a.shape[0] // 2
    ar, ai, br, bi = a[:half], a[half:], b[:half], b[half:]
    return jnp.concatenate([ar * br + ai * bi, ai * br - ar * bi], axis=0)


def pick_kernel(rows_ref, slots_ref, out_ref, pieces):
    block = out_ref.shape[2]

    @pl.when(pl.program_id(0) == 0)
    def _():
        pieces[0], pieces[1], pieces[2] = split3(rows_ref[...])

    hot = rows_hot(rows_ref.shape[1], slots_ref[...])
    picked = dot(pieces[0], hot) + dot(pieces[1], hot) + dot(pieces[2], hot)
    for i in range(CHUNK // block):
        out_ref[i] = picked[:, i * block:(i + 1) * block]


def pick_blocks(rows, slots, peers, block):
    features, length = rows.shape
    steps = peers * block // CHUNK
    return pl.pallas_call(
        pick_kernel,
        grid=(steps,),
        in_specs=[
            pl.BlockSpec((features, length), lambda i: (0, 0)),
            pl.BlockSpec((1, CHUNK), lambda i: (0, i)),
        ],
        out_specs=pl.BlockSpec((CHUNK // block, features, block), lambda i: (i, 0, 0)),
        out_shape=jax.ShapeDtypeStruct((peers, features, block), F32),
        scratch_shapes=[pltpu.VMEM((3, features, length), BF16)],
        compiler_params=params(),
        cost_estimate=cost(6 * features * length * peers * block, 8 * features * peers * block),
        name="pick",
    )(rows, slots)


def relation_kernel(rel_ref, edge_rel_ref, out_ref, pieces):
    count = rel_ref.shape[1]
    padded = pieces.shape[2]

    @pl.when(pl.program_id(0) == 0)
    def _():
        features = rel_ref.shape[0]
        tail = padded - count // LANES * LANES
        for piece, value in enumerate(split3(rel_ref[...])):
            pieces[piece, :, padded - tail:] = jnp.zeros((features, tail), BF16)
            pieces[piece, :, :count] = value

    hot = rows_hot(padded, edge_rel_ref[...])
    out_ref[...] = dot(pieces[0], hot) + dot(pieces[1], hot) + dot(pieces[2], hot)


def relation_rows(relation, edge_relation):
    features, count = relation.shape
    edges = edge_relation.shape[1]
    padded = pl.cdiv(count, LANES) * LANES
    return pl.pallas_call(
        relation_kernel,
        grid=(edges // CHUNK,),
        in_specs=[
            pl.BlockSpec((features, count), lambda i: (0, 0)),
            pl.BlockSpec((1, CHUNK), lambda i: (0, i)),
        ],
        out_specs=pl.BlockSpec((features, CHUNK), lambda i: (0, i)),
        out_shape=jax.ShapeDtypeStruct((features, edges), F32),
        scratch_shapes=[pltpu.VMEM((3, features, padded), BF16)],
        compiler_params=params(),
        cost_estimate=cost(6 * features * padded * edges, 8 * features * edges),
        name="relation_rows",
    )(relation, edge_relation)


def count_kernel(slots_ref, out_ref):
    table_rows = out_ref.shape[2]
    hits = lax.broadcasted_iota(I32, (slots_ref.shape[1], table_rows), 1) == slots_ref[0]
    out_ref[0] = jnp.sum(jnp.where(hits, 1.0, 0.0), axis=0, keepdims=True)


def slot_counts(neg_slots, table_rows):
    spans, negatives = neg_slots.shape
    return pl.pallas_call(
        count_kernel,
        grid=(spans,),
        in_specs=[pl.BlockSpec((1, negatives, 1), lambda i: (i, 0, 0))],
        out_specs=pl.BlockSpec((1, 1, table_rows), lambda i: (i, 0, 0)),
        out_shape=jax.ShapeDtypeStruct((spans, 1, table_rows), F32),
        compiler_params=params(),
        cost_estimate=cost(2 * spans * negatives * table_rows, 512 * spans * negatives),
        name="slot_counts",
    )(neg_slots[:, :, None])


def query_kernel(source_ref, edge_source_ref, rels_ref, heads_ref, columns_ref, rows_ref, pieces):
    peers, features, block = source_ref.shape

    @pl.when(pl.program_id(0) == 0)
    def _():
        for p in range(peers):
            for piece, value in enumerate(split3(source_ref[p])):
                pieces[piece, :, p * block:(p + 1) * block] = value

    hot = rows_hot(peers * block, edge_source_ref[...])
    heads = dot(pieces[0], hot) + dot(pieces[1], hot) + dot(pieces[2], hot)
    heads_ref[...] = heads
    queries = complex_product(heads, rels_ref[...])
    columns_ref[0], columns_ref[1] = split2(queries)
    rows_ref[0], rows_ref[1] = split2(queries.T)


def query_rows(source_blocks, edge_source, rels):
    peers, features, block = source_blocks.shape
    edges = edge_source.shape[1]
    return pl.pallas_call(
        query_kernel,
        grid=(edges // CHUNK,),
        in_specs=[
            pl.BlockSpec((peers, features, block), lambda i: (0, 0, 0)),
            pl.BlockSpec((1, CHUNK), lambda i: (0, i)),
            pl.BlockSpec((features, CHUNK), lambda i: (0, i)),
        ],
        out_specs=[
            pl.BlockSpec((features, CHUNK), lambda i: (0, i)),
            pl.BlockSpec((2, features, CHUNK), lambda i: (0, 0, i)),
            pl.BlockSpec((2, CHUNK, features), lambda i: (0, i, 0)),
        ],
        out_shape=[
            jax.ShapeDtypeStruct((features, edges), F32),
            jax.ShapeDtypeStruct((2, features, edges), BF16),
            jax.ShapeDtypeStruct((2, edges, features), BF16),
        ],
        scratch_shapes=[pltpu.VMEM((3, features, peers * block), BF16)],
        compiler_params=params(),
        cost_estimate=cost(6 * features * peers * block * edges, 20 * features * edges),
        name="query_rows",
    )(source_blocks, edge_source, rels)


def score_kernel(
    live_ref, target_ref, rows_ref, columns_ref, counts_ref, edge_target_ref,
    loss_ref, grad_ref, table_ref, table_grad_ref, total,
):
    peers, features, block = target_ref.shape
    step = pl.program_id(0)

    @pl.when(step == 0)
    def _():
        total[...] = jnp.zeros_like(total)
        for p in range(peers):
            for piece, value in enumerate(split2(target_ref[p])):
                table_ref[piece, :, p * block:(p + 1) * block] = value

    score = (
        dot(rows_ref[0], table_ref[0]) + dot(rows_ref[0], table_ref[1]) + dot(rows_ref[1], table_ref[0])
    )
    counts = counts_ref[0]
    own = lax.broadcasted_iota(I32, score.shape, 1) == edge_target_ref[...]
    pos = jnp.sum(jnp.where(own, score, 0.0), axis=1, keepdims=True)
    peak = jnp.max(jnp.where(counts > 0.0, score, -jnp.inf), axis=1, keepdims=True)
    peak = jnp.maximum(pos, peak)
    weight = counts * jnp.exp(jnp.minimum(score - peak, 0.0))
    pos_weight = jnp.exp(pos - peak)
    sum_all = pos_weight + jnp.sum(weight, axis=1, keepdims=True)
    edge = step * CHUNK + lax.broadcasted_iota(I32, (CHUNK, 1), 0)
    live = jnp.where(edge < live_ref[0], 1.0, 0.0)
    loss_ref[...] = (peak - pos + jnp.log(sum_all)) * live
    scale = live / sum_all
    pos_grad = pos_weight * scale - live
    grad = weight * scale + jnp.where(own, pos_grad, 0.0)
    hi, lo = split2(grad)
    grad_ref[0], grad_ref[1] = hi, lo
    total[...] += dot(columns_ref[0], hi) + dot(columns_ref[0], lo) + dot(columns_ref[1], hi)

    @pl.when(step == pl.num_programs(0) - 1)
    def _():
        for p in range(peers):
            table_grad_ref[p] = total[:, p * block:(p + 1) * block]


def score_spans(live, target_blocks, query_rows_, query_columns, counts, edge_target):
    peers, features, block = target_blocks.shape
    edges = edge_target.shape[0]
    table_rows = peers * block
    per_span = SPAN // CHUNK
    return pl.pallas_call(
        score_kernel,
        grid=(edges // CHUNK,),
        in_specs=[
            pl.BlockSpec(memory_space=pltpu.SMEM),
            pl.BlockSpec((peers, features, block), lambda i: (0, 0, 0)),
            pl.BlockSpec((2, CHUNK, features), lambda i: (0, i, 0)),
            pl.BlockSpec((2, features, CHUNK), lambda i: (0, 0, i)),
            pl.BlockSpec((1, 1, table_rows), lambda i: (i // per_span, 0, 0)),
            pl.BlockSpec((CHUNK, 1), lambda i: (i, 0)),
        ],
        out_specs=[
            pl.BlockSpec((CHUNK, 1), lambda i: (i, 0)),
            pl.BlockSpec((2, CHUNK, table_rows), lambda i: (0, i, 0)),
            pl.BlockSpec((2, features, table_rows), lambda i: (0, 0, 0)),
            pl.BlockSpec((peers, features, block), lambda i: (0, 0, 0)),
        ],
        out_shape=[
            jax.ShapeDtypeStruct((edges, 1), F32),
            jax.ShapeDtypeStruct((2, edges, table_rows), BF16),
            jax.ShapeDtypeStruct((2, features, table_rows), BF16),
            jax.ShapeDtypeStruct((peers, features, block), F32),
        ],
        scratch_shapes=[pltpu.VMEM((features, table_rows), F32)],
        compiler_params=params(),
        cost_estimate=cost(12 * features * table_rows * edges, 30 * features * edges),
        name="score_spans",
    )(live, target_blocks, query_rows_, query_columns, counts, edge_target)


def edge_grad_kernel(
    table_ref, grad_ref, heads_ref, rels_ref, edge_rel_ref, edge_source_ref,
    rel_grad_ref, source_grad_ref, rel_total, source_total,
):
    step = pl.program_id(0)
    parts, _, width = rel_grad_ref.shape
    peers, _, block = source_grad_ref.shape

    @pl.when(step == 0)
    def _():
        rel_total[...] = jnp.zeros_like(rel_total)
        source_total[...] = jnp.zeros_like(source_total)

    query_grad = (
        dot_nt(table_ref[0], grad_ref[0]) + dot_nt(table_ref[0], grad_ref[1]) + dot_nt(table_ref[1], grad_ref[0])
    )
    hi, lo = split2(conj_product(query_grad, heads_ref[...]))
    hot = columns_hot(edge_rel_ref[...], parts * width)
    rel_total[...] += dot(hi, hot) + dot(lo, hot)
    hi, lo = split2(conj_product(query_grad, rels_ref[...]))
    hot = columns_hot(edge_source_ref[...], peers * block)
    source_total[...] += dot(hi, hot) + dot(lo, hot)

    @pl.when(step == pl.num_programs(0) - 1)
    def _():
        for p in range(parts):
            rel_grad_ref[p] = rel_total[:, p * width:(p + 1) * width]
        for p in range(peers):
            source_grad_ref[p] = source_total[:, p * block:(p + 1) * block]


def edge_grads(table, grad, heads, rels, edge_relation, edge_source, parts, width, peers, block):
    _, features, table_rows = table.shape
    edges = heads.shape[1]
    return pl.pallas_call(
        edge_grad_kernel,
        grid=(edges // CHUNK,),
        in_specs=[
            pl.BlockSpec((2, features, table_rows), lambda i: (0, 0, 0)),
            pl.BlockSpec((2, CHUNK, table_rows), lambda i: (0, i, 0)),
            pl.BlockSpec((features, CHUNK), lambda i: (0, i)),
            pl.BlockSpec((features, CHUNK), lambda i: (0, i)),
            pl.BlockSpec((CHUNK, 1), lambda i: (i, 0)),
            pl.BlockSpec((CHUNK, 1), lambda i: (i, 0)),
        ],
        out_specs=[
            pl.BlockSpec((parts, features, width), lambda i: (0, 0, 0)),
            pl.BlockSpec((peers, features, block), lambda i: (0, 0, 0)),
        ],
        out_shape=[
            jax.ShapeDtypeStruct((parts, features, width), F32),
            jax.ShapeDtypeStruct((peers, features, block), F32),
        ],
        scratch_shapes=[
            pltpu.VMEM((features, parts * width), F32),
            pltpu.VMEM((features, peers * block), F32),
        ],
        compiler_params=params(),
        cost_estimate=cost(16 * features * table_rows * edges, 30 * features * edges),
        name="edge_grads",
    )(table, grad, heads, rels, edge_relation, edge_source)


def put_back(received_ref, slots_ref, rows):
    peers, _, block = received_ref.shape
    total = None
    for p in range(peers):
        hi, lo = split2(received_ref[p])
        hot = columns_hot(slots_ref[p * block:(p + 1) * block, :], rows)
        term = dot(hi, hot) + dot(lo, hot)
        total = term if total is None else total + term
    return total


def target_home_kernel(received_ref, slots_ref, out_ref):
    out_ref[...] = put_back(received_ref, slots_ref, out_ref.shape[1])


def target_home(received, slots, rows):
    features = received.shape[1]
    return pl.pallas_call(
        target_home_kernel,
        in_specs=[WHOLE, WHOLE],
        out_specs=WHOLE,
        out_shape=jax.ShapeDtypeStruct((features, rows), F32),
        compiler_params=pltpu.CompilerParams(vmem_limit_bytes=VMEM_LIMIT),
        cost_estimate=cost(4 * features * rows * slots.shape[0], 8 * features * slots.shape[0]),
        name="target_home",
    )(received, slots)


def adagrad(params_, state, gradient):
    new_state = state + jnp.mean(gradient * gradient, axis=0, keepdims=True)
    return params_ - learn_rate * gradient / jnp.sqrt(new_state)


def entity_kernel(received_ref, slots_ref, other_ref, entity_ref, state_ref, out_ref):
    gradient = other_ref[...] + put_back(received_ref, slots_ref, out_ref.shape[1])
    out_ref[...] = adagrad(entity_ref[...], state_ref[...], gradient)


def entity_update(received, slots, other, entity, state):
    features, rows = entity.shape
    return pl.pallas_call(
        entity_kernel,
        in_specs=[WHOLE] * 5,
        out_specs=WHOLE,
        out_shape=jax.ShapeDtypeStruct((features, rows), F32),
        compiler_params=pltpu.CompilerParams(vmem_limit_bytes=VMEM_LIMIT),
        cost_estimate=cost(4 * features * rows * slots.shape[0], 8 * features * slots.shape[0]),
        name="entity_update",
    )(received, slots, other, entity, state)


def swapped(value, axis, bit):
    count = lax.axis_size(axis)
    return lax.ppermute(value, axis, [(i, i ^ bit) for i in range(count)])


def passed_along(value, axis, by):
    count = lax.axis_size(axis)
    return lax.ppermute(value, axis, [(i, (i + by) % count) for i in range(count)])


def relation_sum(parts):
    groups, features, width = parts.shape
    half = features // 2
    shards = lax.axis_size("shard")
    chips = shards // 2
    core = lax.axis_index("shard") % 2
    lines = [[chip * 2 + c for chip in range(chips)] for c in range(2)]
    halves = parts.reshape(groups, 2, half, width)
    kept = lax.dynamic_index_in_dim(halves, core, 1, keepdims=False)
    sent = lax.dynamic_index_in_dim(halves, 1 - core, 1, keepdims=False)
    mine = kept + swapped(sent, "shard", 1)
    mine = jnp.sum(lax.all_to_all(mine, "group", 0, 0, tiled=True), axis=0)
    slices = mine.reshape(chips, half // chips, width)
    slices = lax.all_to_all(slices, "shard", 0, 0, axis_index_groups=lines, tiled=True)
    piece = jnp.sum(slices, axis=0)
    slices = lax.all_to_all(
        jnp.broadcast_to(piece[None], slices.shape), "shard", 0, 0, axis_index_groups=lines, tiled=True
    )
    mine = slices.reshape(half, width)
    mine = lax.all_to_all(
        jnp.broadcast_to(mine[None], (groups, half, width)), "group", 0, 0, tiled=True
    )
    other = swapped(mine, "shard", 1)
    low = jnp.where(core == 0, mine, other)
    high = jnp.where(core == 0, other, mine)
    return jnp.concatenate([low, high], axis=1).transpose(1, 0, 2).reshape(features, groups * width)


def on_device(
    entity, entity_state, relation, relation_state, src_send, dst_send,
    edge_source, edge_relation, edge_target, neg_slots, edge_count,
):
    rows, features = entity.shape
    relations = relation.shape[0]
    peers, block = src_send.shape[1:]
    edges = edge_source.shape[0]
    table_rows = peers * block
    groups = lax.axis_size("group")
    width = pl.cdiv(relations, groups * LANES) * LANES
    entity_t, relation_t = entity.T, relation.T

    exchange = functools.partial(
        lax.all_to_all, axis_name="shard", split_axis=0, concat_axis=0, tiled=True
    )
    source_blocks = exchange(pick_blocks(entity_t, src_send.reshape(1, -1), peers, block))
    shifted = passed_along(pick_blocks(entity_t, dst_send.reshape(1, -1), peers, block), "group", -1)
    target_blocks = exchange(shifted)
    rels = relation_rows(relation_t, edge_relation.reshape(1, -1))
    counts = slot_counts(neg_slots, table_rows)
    heads, query_columns, query_rows_ = query_rows(source_blocks, edge_source.reshape(1, -1), rels)
    loss, grad, table, table_grad = score_spans(
        edge_count, target_blocks, query_rows_, query_columns, counts, edge_target.reshape(-1, 1)
    )
    home = passed_along(exchange(table_grad), "group", 1)
    rel_parts, source_grad = edge_grads(
        table, grad, heads, rels, edge_relation.reshape(-1, 1), edge_source.reshape(-1, 1),
        groups, width, peers, block,
    )
    rel_total = relation_sum(rel_parts)[:, :relations]
    returned = exchange(source_grad)
    target_part = target_home(home, dst_send.reshape(-1, 1), rows)
    entity_new = entity_update(
        returned, src_send.reshape(-1, 1), target_part, entity_t, entity_state.reshape(1, -1)
    )
    relation_new = adagrad(relation_t, relation_state.reshape(1, -1), rel_total)
    return entity_new.T, relation_new.T, loss.reshape(-1)


def solution(mesh):
    both = ("group", "shard")
    return jax.shard_map(
        on_device,
        mesh=mesh,
        in_specs=(
            P(both, None), P(both), P(), P(), P(both, None, None), P(both, None, None),
            P(both), P(both), P(both), P(both, None), P(both),
        ),
        out_specs=(P(both, None), P(), P(both)),
        check_vma=False,
    )
```

time: 458 us -> 309 us (0.67)
  waiting for transfers between devices: 231 us -> 130 us
  other arithmetic: 83.7 us -> 5.85 us
  Pallas kernels: 0 us -> 68.7 us
  blocking collectives: 0 us -> 64.2 us
  local copies, waits for them, and re-layouts: 68.6 us -> 15.6 us
  matrix products: 29 us -> 0 us
  between operations: 15.5 us -> 1.43 us
    psum x1 -> x0, waiting for transfers between devices: 156 us -> none  [on_device(): relation_total = lax.psum(relation_part, ('group', 'shard'))]
    pallas_call x0 -> x9, Pallas kernels: none -> 68.7 us  [the longest x1 18.3 us: edge_grads(): pl.pallas_call(edge_grad_kernel, grid=(edges // CHUNK,), in_specs=[pl.Blo...]
    all_to_all x0 -> x4, blocking collectives: none -> 64.2 us  [the longest x1 21 us: relation_sum(): mine = jnp.sum(lax.all_to_all(mine, 'group', 0, 0, tiled=True), axis=0)]
    scatter-add x7 -> x0, other arithmetic: 62.5 us -> none  [the longest x2 20.2 us: span_turn(): target_grad = target_grad.at[slots].add(negative_grad)]
    ppermute x2, waiting for transfers between devices: 36.1 us -> 71.7 us  [passed_along(): lax.ppermute(value, axis, [(i, (i + by) % count) for i in range(count)])]
    gather x9 -> x0, local copies, waits for them, and re-layouts: 34.8 us -> none  [the longest x2 9.71 us: span_turn(): target_table[slots]]
    dot_general x6 -> x0, matrix products: 29 us -> none  [the longest x2 10.9 us: span_terms(): neg_score = jnp.dot(queries, negatives.T, precision=lax.Precision.HIGHEST)]
    all_to_all x4, waiting for transfers between devices: 39.4 us -> 55.3 us  [the longest x1 39.1 us: on_device(): home = passed_along(exchange(table_grad), 'group', 1)]
  transfers between devices with their start and end apart: 7 -> 8, of which waited for: 4 -> 5; matrix products, arithmetic and copies ran while one was open for 15% -> 2% of each run, Pallas kernels for 0% -> 10%
where the time goes in v1:
time: 309 us; the launch traced here: 308 us
  waiting for transfers between devices  130 us (42%)
  Pallas kernels  68.7 us (22%)
  blocking collectives  64.2 us (21%)
  starting transfers between devices  21.7 us (7%)
  local copies, waits for them, and re-layouts  15.6 us (5%)
  other arithmetic  5.85 us (2%)
    ppermute x2, waiting for transfers between devices, passed_along(): lax.ppermute(value, axis, [(i, (i + by) % count) for i in range(count)])  71.7 us
    all_to_all x1, waiting for transfers between devices, on_device(): home = passed_along(exchange(table_grad), 'group', 1)  39.1 us
    all_to_all x1, blocking collectives, relation_sum(): mine = jnp.sum(lax.all_to_all(mine, 'group', 0, 0, tiled=True), axis=0)  21 us
    all_to_all x1, blocking collectives, relation_sum(): lax.all_to_all(jnp.broadcast_to(mine[None], (groups, half, width)), 'grou...  18.7 us
    pallas_call x1, Pallas kernels, edge_grads(): pl.pallas_call(edge_grad_kernel, grid=(edges // CHUNK,), in_specs=[pl.Blo...  18.3 us
    all_to_all x1, waiting for transfers between devices, on_device(): target_blocks = exchange(shifted)  16.2 us
    pallas_call x1, Pallas kernels, score_spans(): pl.pallas_call(score_kernel, grid=(edges // CHUNK,), in_specs=[pl.BlockSp...  14 us
    all_to_all x1, blocking collectives, relation_sum(): lax.all_to_all(jnp.broadcast_to(piece[None], slices.shape), 'shard', 0, 0...  12.3 us
  transfers between devices with their start and end apart: 8, of which 5 were waited for; matrix products, arithmetic and copies ran while one was open for 2% of the time, Pallas kernels for 10%

profile of v1, /device:TPU:0, one launch (start us, length us, event | category | flops | bytes accessed | tf_op | source)
XLA Modules:
  0.0 307.7 jit_solution(7014144399783863515)
XLA Ops:
  0.6 4.6 %pick.3 = f32[8,400,128]{2,1,0:T(8,128)} custom-call(f32[400,512]{1,0:T(8,128)} %bitcast.31, s32[1,1024]{1,0:T(1,128)} %bitcast.41), custom_call_target="tpu_custom_call" | custom-call | flops 1258291200 | bytes 3276800 | tf_op jit(solution)/shard_map/pick/pallas_call | solution.py:89
  5.2 6.4 %all-to-all-start.1 = ((f32[8,400,128]{2,1,0:T(8,128)}), f32[8,400,128]{2,1,0:T(8,128)S(1)}, u32[]{:S(2)}, u32[]{:S(2)}) async-start(f32[8,400,128]{2,1,0:T(8,128)} %pick.3), calls=%async_computation.1 | async-start | bytes 3276800 | tf_op jit(solution)/shard_map/all_to_all | solution.py:450
  11.5 4.5 %pick.2 = f32[8,400,128]{2,1,0:T(8,128)} custom-call(f32[400,512]{1,0:T(8,128)} %bitcast.32, s32[1,1024]{1,0:T(1,128)} %bitcast.43), custom_call_target="tpu_custom_call" | custom-call | flops 1258291200 | bytes 3276800 | tf_op jit(solution)/shard_map/pick/pallas_call | solution.py:89
  16.1 2.5 collective-permute-start
  18.6 36.1 %collective-permute-done = f32[8,400,128]{2,1,0:T(8,128)} collective-permute-done((f32[8,400,128]{2,1,0:T(8,128)}, f32[8,400,128]{2,1,0:T(8,128)}, u32[]{:S(2)}, u32[]{:S(2)}) %collective-permute-start) | collective-permute-done | bytes 1638432 | tf_op jit(solution)/shard_map/ppermute | solution.py:403
  54.7 1.2 copy-done.3
  55.8 4.7 %all-to-all-start = ((f32[8,400,128]{2,1,0:T(8,128)}), f32[8,400,128]{2,1,0:T(8,128)S(1)}, u32[]{:S(2)}, u32[]{:S(2)}) async-start(f32[8,400,128]{2,1,0:T(8,128)} %collective-permute-done), calls=%async_computation | async-start | bytes 3276800 | tf_op jit(solution)/shard_map/all_to_all | solution.py:452
  61.2 1.3 copy.20.slots_ref
  62.5 1.0 copy.21.edge_target_ref
  63.6 1.0 copy.22.edge_rel_ref
  64.6 1.0 copy.23.edge_source_ref
  65.6 2.6 slot_counts.1.counts_ref
  68.2 7.6 %relation_rows.1.rels_ref = f32[400,1024]{1,0:T(8,128)} custom-call(f32[400,1345]{1,0:T(8,128)} %bitcast.30, s32[1,1024]{1,0:T(1,128)} %bitcast.37), custom_call_target="tpu_custom_call" | custom-call | flops 3460300800 | bytes 3276800 | tf_op jit(solution)/shard_map/relation_rows/pallas_call | solution.py:125
  75.8 7.7 %query_rows.1 = (f32[400,1024]{1,0:T(8,128)}, bf16[2,400,1024]{2,1,0:T(8,128)(2,1)}, bf16[2,1024,400]{2,1,0:T(8,128)(2,1)}) custom-call(f32[8,400,128]{2,1,0:T(8,128)} %copy-done.3, s32[1,1024]{1,0:T(1,128)} %bitcast.39, f32[400,1024]{1,0:T(8,128)} %relation_rows.1.rels_ref), custom_call_target="tpu_custom_call" | custom-call | flops 2516582400 | bytes 8192000 | tf_op jit(solution)/shard_map/query_rows/pallas_call | solution.py:181
  83.6 16.2 %all-to-all-done.target_ref = f32[8,400,128]{2,1,0:T(8,128)S(1)} async-done(((f32[8,400,128]{2,1,0:T(8,128)}), f32[8,400,128]{2,1,0:T(8,128)S(1)}, u32[]{:S(2)}, u32[]{:S(2)}) %all-to-all-start) | async-done | bytes 1638432 | tf_op jit(solution)/shard_map/all_to_all | solution.py:452
  99.7 1.2 copy-done.4
  100.9 14.0 %score_spans.1 = (f32[1024,1]{1,0:T(8,128)}, bf16[2,1024,1024]{2,1,0:T(8,128)(2,1)}, bf16[2,400,1024]{2,1,0:T(8,128)(2,1)}, f32[8,400,128]{2,1,0:T(8,128)}) custom-call(s32[1]{0:T(128)S(6)} %copy.28.live_ref, f32[8,400,128]{2,1,0:T(8,128)} %copy-done.4, bf16[2,1024,400]{2,1,0:T(8,128)(2,1)} %get-tuple-element.12.rows_ref, ...), custom_call_target="tpu_custom_call" | custom-call | flops 5033164800 | bytes 12288000 | tf_op jit(solution)/shard_map/score_spans/pallas_call | solution.py:252
  114.9 18.3 %edge_grads.1 = (f32[4,400,384]{2,1,0:T(8,128)}, f32[8,400,128]{2,1,0:T(8,128)}) custom-call(bf16[2,400,1024]{2,1,0:T(8,128)(2,1)} %get-tuple-element.14.table_ref, bf16[2,1024,1024]{2,1,0:T(8,128)(2,1)} %get-tuple-element.15.grad_ref, f32[400,1024]{1,0:T(8,128)} %get-tuple-element.16.heads_ref, f32[400,1024]{1,0:T(8,128)} %relation_rows.1.rels_ref, ...), custom_call_target="tpu_custom_call" | custom-call | flops 6710886400 | bytes 12288000 | tf_op jit(solution)/shard_map/edge_grads/pallas_call | solution.py:316
  133.2 2.6 dynamic-slice_bitcast_fusion
  135.8 3.3 %collective-permute-done.2 = f32[4,200,384]{2,1,0:T(8,128)} collective-permute-done((f32[4,200,384]{2,1,0:T(8,128)}, f32[4,200,384]{2,1,0:T(8,128)}, u32[]{:S(2)}, u32[]{:S(2)}) %collective-permute-start.2) | collective-permute-done | bytes 1228832 | tf_op jit(solution)/shard_map/ppermute | solution.py:398
  139.1 1.4 bitcast_add_fusion
  140.5 21.0 %all_to_all.40 = f32[4,200,384]{2,1,0:T(8,128)S(1)} all-to-all(f32[4,200,384]{2,1,0:T(8,128)S(1)} %bitcast_add_fusion), channel_id=1, replica_groups=mesh['group'=4,'shard'=8] {'group'}, dimensions={0} | all-to-all | bytes 2457600 | tf_op jit(solution)/shard_map/all_to_all | solution.py:417
  161.5 0.1 reduce_sum.27
  161.6 12.2 %all_to_all.41 = f32[4,50,384]{2,1,0:T(8,128)S(1)} all-to-all(f32[4,50,384]{2,1,0:T(8,128)S(1)} %reshape.66), channel_id=1, replica_groups={{0,2,4,6},{1,3,5,7},{8,10,12,14},{9,11,13,15},{16,18,20,22},{17,19,21,2..., dimensions={0} | all-to-all | bytes 614400 | tf_op jit(solution)/shard_map/all_to_all | solution.py:419
  173.8 12.3 %all_to_all.42 = f32[4,50,384]{2,1,0:T(8,128)S(1)} all-to-all(f32[4,50,384]{2,1,0:T(8,128)S(1)} %broadcast_in_dim.18), channel_id=1, replica_groups={{0,2,4,6},{1,3,5,7},{8,10,12,14},{9,11,13,15},{16,18,20,22},{17,19,21,2..., dimensions={0} | all-to-all | bytes 614400 | tf_op jit(solution)/shard_map/all_to_all | solution.py:421
  186.1 3.6 %all-to-all-start.3 = ((f32[8,400,128]{2,1,0:T(8,128)}), f32[8,400,128]{2,1,0:T(8,128)S(1)}, u32[]{:S(2)}, u32[]{:S(2)}) async-start(f32[8,400,128]{2,1,0:T(8,128)} %get-tuple-element.18), calls=%async_computation.3 | async-start | bytes 3276800 | tf_op jit(solution)/shard_map/all_to_all | solution.py:459
  189.8 39.1 %all-to-all-done.3 = f32[8,400,128]{2,1,0:T(8,128)S(1)} async-done(((f32[8,400,128]{2,1,0:T(8,128)}), f32[8,400,128]{2,1,0:T(8,128)S(1)}, u32[]{:S(2)}, u32[]{:S(2)}) %all-to-all-start.3) | async-done | bytes 1638432 | tf_op jit(solution)/shard_map/all_to_all | solution.py:459
  228.9 1.2 copy-done.5
  230.0 0.1 broadcast_in_dim.20
  230.1 18.7 %all_to_all.43 = f32[4,200,384]{2,1,0:T(8,128)S(1)} all-to-all(f32[4,200,384]{2,1,0:T(8,128)S(1)} %broadcast_in_dim.20), channel_id=1, replica_groups=mesh['group'=4,'shard'=8] {'group'}, dimensions={0} | all-to-all | bytes 2457600 | tf_op jit(solution)/shard_map/all_to_all | solution.py:425
  248.8 3.7 %all-to-all-start.2 = ((f32[8,400,128]{2,1,0:T(8,128)}), f32[8,400,128]{2,1,0:T(8,128)S(1)}, u32[]{:S(2)}, u32[]{:S(2)}) async-start(f32[8,400,128]{2,1,0:T(8,128)} %get-tuple-element.17), calls=%async_computation.2 | async-start | bytes 3276800 | tf_op jit(solution)/shard_map/all_to_all | solution.py:465
  252.5 0.7 collective-permute-start.1
  253.3 0.1 collective-permute-start.3
  253.3 1.0 copy.25.slots_ref
  254.4 1.0 copy.24.slots_ref
  255.4 0.8 reduce
  256.2 35.6 %collective-permute-done.1.received_ref = f32[8,400,128]{2,1,0:T(8,128)} collective-permute-done((f32[8,400,128]{2,1,0:T(8,128)}, f32[8,400,128]{2,1,0:T(8,128)}, u32[]{:S(2)}, u32[]{:S(2)}) %collective-permute-start.1) | collective-permute-done | bytes 1638432 | tf_op jit(solution)/shard_map/ppermute | solution.py:403
  291.8 4.3 %target_home.1.other_ref = f32[400,512]{1,0:T(8,128)} custom-call(f32[8,400,128]{2,1,0:T(8,128)} %collective-permute-done.1.received_ref, s32[1024,1]{1,0:T(8,128)} %copy.24.slots_ref), custom_call_target="tpu_custom_call" | custom-call | flops 838860800 | bytes 3276800 | tf_op jit(solution)/shard_map/target_home/pallas_call | solution.py:362
  296.2 1.2 copy-done
  297.4 5.0 %entity_update.1 = f32[400,512]{1,0:T(8,128)} custom-call(f32[8,400,128]{2,1,0:T(8,128)} %copy-done, s32[1024,1]{1,0:T(8,128)} %copy.25.slots_ref, f32[400,512]{1,0:T(8,128)} %target_home.1.other_ref, f32[400,512]{1,0:T(8,128)} %bitcast.33, f32[1,512]{1,0:T(1,128)} %bitcast.45), custom_call_target="tpu_custom_call" | custom-call | flops 838860800 | bytes 3276800 | tf_op jit(solution)/shard_map/entity_update/pallas_call | solution.py:385
  302.4 1.4 broadcast_select_fusion.1
  303.9 0.2 maximum_bitcast_fusion
  304.0 0.3 copy.27
  304.4 0.0 copy-start.8
  304.4 0.2 multiply_reduce_fusion
  304.6 0.4 copy-done.8
  305.1 0.9 copy-done.2
  306.0 1.7 subtract_bitcast_fusion
  (30 shorter events, 0.2 us)
Async XLA Ops:
  5.2 49.5 %all-to-all-start.1 = ((f32[8,400,128]{2,1,0:T(8,128)}), f32[8,400,128]{2,1,0:T(8,128)S(1)}, u32[]{:S(2)}, u32[]{:S(2)}) async-start(f32[8,400,128]{2,1,0:T(8,128)} %pick.3), calls=%async_computation.1 | async-start | bytes 3276800 | tf_op jit(solution)/shard_map/all_to_all | solution.py:450
  16.1 45.1 %copy-start.7 = (s32[2,1000]{1,0:T(2,128)S(1)}, s32[2,1000]{1,0:T(2,128)}, u32[]{:S(2)}) copy-start(s32[2,1000]{1,0:T(2,128)} %param.20) | copy-start | bytes 24004
  16.1 46.5 %copy-start.9 = (s32[1024]{0:T(1024)S(1)}, s32[1024]{0:T(1024)}, u32[]{:S(2)}) copy-start(s32[1024]{0:T(1024)} %param.19) | copy-start | bytes 12292
  16.1 47.5 %copy-start.10 = (s32[1024]{0:T(1024)S(1)}, s32[1024]{0:T(1024)}, u32[]{:S(2)}) copy-start(s32[1024]{0:T(1024)} %param.18) | copy-start | bytes 12292
  16.1 38.6 %collective-permute-start = (f32[8,400,128]{2,1,0:T(8,128)}, f32[8,400,128]{2,1,0:T(8,128)}, u32[]{:S(2)}, u32[]{:S(2)}) collective-permute-start(f32[8,400,128]{2,1,0:T(8,128)} %pick.2), channel_id=1, source_target_pairs={{0,24},{8,0},{16,8},{24,16},{1,25},{9,1},{17,9},{25,17},{2,26},{10... | collective-permute-start | bytes 4915208 | tf_op jit(solution)/shard_map/ppermute | solution.py:403
  54.7 1.2 copy-start.3
  55.8 43.9 %all-to-all-start = ((f32[8,400,128]{2,1,0:T(8,128)}), f32[8,400,128]{2,1,0:T(8,128)S(1)}, u32[]{:S(2)}, u32[]{:S(2)}) async-start(f32[8,400,128]{2,1,0:T(8,128)} %collective-permute-done), calls=%async_computation | async-start | bytes 3276800 | tf_op jit(solution)/shard_map/all_to_all | solution.py:452
  60.5 4.1 %copy-start.11 = (s32[1024]{0:T(1024)S(1)}, s32[1024]{0:T(1024)}, u32[]{:S(2)}) copy-start(s32[1024]{0:T(1024)} %param.17) | copy-start | bytes 12292
  99.7 1.2 copy-start.4
  133.2 5.8 %copy-start.1 = (f32[4,400,384]{2,1,0:T(8,128)S(1)}, f32[4,400,384]{2,1,0:T(8,128)}, u32[]{:S(2)}) copy-start(f32[4,400,384]{2,1,0:T(8,128)} %get-tuple-element.19) | copy-start | bytes 7372804
  135.8 3.3 %collective-permute-start.2 = (f32[4,200,384]{2,1,0:T(8,128)}, f32[4,200,384]{2,1,0:T(8,128)}, u32[]{:S(2)}, u32[]{:S(2)}) collective-permute-start(f32[4,200,384]{2,1,0:T(8,128)} %dynamic-slice_bitcast_fusion), channel_id=1, source_target_pairs={{0,1},{1,0},{2,3},{3,2},{4,5},{5,4},{6,7},{7,6},{8,9},{9,8},{10,11... | collective-permute-start | bytes 3686408 | tf_op jit(solution)/shard_map/ppermute | solution.py:398
  186.1 42.7 %all-to-all-start.3 = ((f32[8,400,128]{2,1,0:T(8,128)}), f32[8,400,128]{2,1,0:T(8,128)S(1)}, u32[]{:S(2)}, u32[]{:S(2)}) async-start(f32[8,400,128]{2,1,0:T(8,128)} %get-tuple-element.18), calls=%async_computation.3 | async-start | bytes 3276800 | tf_op jit(solution)/shard_map/all_to_all | solution.py:459
  228.8 1.2 copy-start.5
  248.8 4.6 %copy-start.12 = (s32[1,8,128]{2,1,0:T(8,128)S(1)}, s32[1,8,128]{2,1,0:T(8,128)}, u32[]{:S(2)}) copy-start(s32[1,8,128]{2,1,0:T(8,128)} %param.15) | copy-start | bytes 12292
  248.8 5.6 %copy-start.13 = (s32[1,8,128]{2,1,0:T(8,128)S(1)}, s32[1,8,128]{2,1,0:T(8,128)}, u32[]{:S(2)}) copy-start(s32[1,8,128]{2,1,0:T(8,128)} %param.16) | copy-start | bytes 12292
  248.8 6.6 %copy-start.6 = (f32[1024,1]{1,0:T(8,128)S(1)}, f32[1024,1]{1,0:T(8,128)}, u32[]{:S(2)}) copy-start(f32[1024,1]{1,0:T(8,128)} %get-tuple-element.20) | copy-start | bytes 12292
  248.8 47.4 %all-to-all-start.2 = ((f32[8,400,128]{2,1,0:T(8,128)}), f32[8,400,128]{2,1,0:T(8,128)S(1)}, u32[]{:S(2)}, u32[]{:S(2)}) async-start(f32[8,400,128]{2,1,0:T(8,128)} %get-tuple-element.17), calls=%async_computation.2 | async-start | bytes 3276800 | tf_op jit(solution)/shard_map/all_to_all | solution.py:465
  252.5 39.3 %collective-permute-start.1 = (f32[8,400,128]{2,1,0:T(8,128)}, f32[8,400,128]{2,1,0:T(8,128)}, u32[]{:S(2)}, u32[]{:S(2)}) collective-permute-start(f32[8,400,128]{2,1,0:T(8,128)} %copy-done.5), channel_id=1, source_target_pairs={{0,8},{8,16},{16,24},{24,0},{1,9},{9,17},{17,25},{25,1},{2,10},{10... | collective-permute-start | bytes 4915208 | tf_op jit(solution)/shard_map/ppermute | solution.py:403
  253.3 49.1 %collective-permute-start.3 = (f32[4,200,384]{2,1,0:T(8,128)S(1)}, f32[4,200,384]{2,1,0:T(8,128)}, u32[]{:S(2)}, u32[]{:S(2)}) collective-permute-start(f32[4,200,384]{2,1,0:T(8,128)S(1)} %all_to_all.43), channel_id=1, source_target_pairs={{0,1},{1,0},{2,3},{3,2},{4,5},{5,4},{6,7},{7,6},{8,9},{9,8},{10,11... | collective-permute-start | bytes 3686408 | tf_op jit(solution)/shard_map/ppermute | solution.py:398
  296.2 1.2 copy-start
  304.4 0.7 copy-start.8
  304.4 1.6 copy-start.2
